TPU v7x, 32 devices: a whole 2x2x4 slice. The times are simulated.
32 devices in a mesh: row: 2 (over y), col: 8 (over z, x), depth: 2 (over core).
Axes of the slice: x: 2, y: 2, z: 4, core: 2. Of those that a mesh axis runs over, the one named last changes fastest.
Arguments:
- a_tiles: bfloat16 [2, 16, 8, 2, 128, 128], P('row', ('col', 'depth')), may hold values from -1.5 to 1.5
- a_cols: int32 [2, 16, 8, 2], P('row', ('col', 'depth')), may hold values from 0 to 15, as said below
- a_count: int32 [2, 16, 8], P('row', ('col', 'depth')), may hold values from 0 to 2, as said below
- b_tiles: bfloat16 [4, 2, 2, 8, 16, 1, 128, 128], P(None, 'row', 'depth', 'col'), may hold values from -1.5 to 1.5
- b_cols: int32 [4, 2, 2, 8, 16, 1], P(None, 'row', 'depth', 'col'), may hold values from 0 to 11, as said below
- b_count: int32 [4, 2, 2, 8, 16], P(None, 'row', 'depth', 'col'), may hold values from 0 to 1, as said below
Outputs:
- product: bfloat16 [2048, 12288], P(('row', 'depth'), 'col')
Inputs may be any that keep to these rules, and one draw needn't show every extreme that they name: The entries of a_cols for one row group, inner panel and block row are distinct. `a_count`: some block row holds 2 blocks in every draw. The entries of b_cols for one inner block row are distinct. `b_count`: some inner block row holds 1 block in every draw.
All inputs are finite; a program needn't handle non-finite values.
Results may differ from a plain program's by a relative error of at most 0.001.
Values may be sent and summed in bfloat16 or wider, within the bound.
A program may use at most 128 MiB of HBM per device.

v0:
```python
import math
import jax
import jax.numpy as jnp
from jax import lax
from jax.sharding import PartitionSpec as P

BC = 12
SHIFTS = 4


def for_sending(array):
    return jax.tree.map(lambda a: a.astype(jnp.bfloat16) if a.dtype == jnp.float32 else a, array)


def shifted(value, axis, steps):
    count = lax.axis_size(axis)
    pairs = [(source, (source + steps) % count) for source in range(count)]
    return lax.ppermute(value, axis, pairs)


def dense_panel(tiles_b, cols_b, count_b, width):
    slot_ids = lax.broadcasted_iota(jnp.int32, cols_b.shape, 1)
    valid_slot = slot_ids < count_b[:, None]
    targets = lax.broadcasted_iota(jnp.int32, (1, 1, width), 2)
    placing = jnp.logical_and(cols_b[:, :, None] == targets, valid_slot[:, :, None]).astype(
        jnp.bfloat16
    )
    spread = jnp.einsum("kuc,kuab->kacb", placing, tiles_b, preferred_element_type=jnp.float32)
    inner_blocks = tiles_b.shape[0]
    tile_size = tiles_b.shape[2]
    return spread.astype(jnp.bfloat16).reshape(inner_blocks, tile_size, width * tile_size)


def panel_product(tiles_a, cols_a, count_a, rows_dense):
    block_rows = tiles_a.shape[0]
    per_row = tiles_a.shape[1]
    tile_size = tiles_a.shape[2]
    slot_ids = lax.broadcasted_iota(jnp.int32, cols_a.shape, 1)
    valid_slot = slot_ids < count_a[:, None]
    masked = jnp.where(valid_slot[:, :, None, None], tiles_a, jnp.zeros_like(tiles_a))
    group_rows = math.gcd(block_rows, 4)

    def one_group(pieces):
        tiles_part, cols_part = pieces
        chosen = jnp.take(rows_dense, cols_part, axis=0)
        return jnp.einsum("rtab,rtbn->ran", tiles_part, chosen, preferred_element_type=jnp.float32)

    grouped = lax.map(
        one_group,
        (
            masked.reshape(block_rows // group_rows, group_rows, per_row, tile_size, tile_size),
            cols_a.reshape(block_rows // group_rows, group_rows, per_row),
        ),
    )
    return grouped.reshape(block_rows, tile_size, rows_dense.shape[2])


def roll_slots(stack, offset):
    slot_total = stack[0].shape[0]
    return tuple(
        (
            lax.dynamic_slice_in_dim(
                jnp.concatenate([member, member], 0), offset % slot_total, slot_total, 0
            )
            for member in stack
        )
    )


def select_if(flag, fresh, stale):
    return tuple((jnp.where(flag, new_part, old_part) for new_part, old_part in zip(fresh, stale)))


def local(a_tiles, a_cols, a_count, b_tiles, b_cols, b_count):
    rows_axis = lax.axis_size("row")
    cols_axis = lax.axis_size("col")
    row_group = lax.axis_index("row")
    col_group = lax.axis_index("col")
    tiles_a = a_tiles[0, 0]
    cols_a = a_cols[0, 0]
    count_a = a_count[0, 0]
    tiles_b = b_tiles[:, 0, 0, 0]
    cols_b = b_cols[:, 0, 0, 0]
    count_b = b_count[:, 0, 0, 0]
    for bit_pos in range((rows_axis - 1).bit_length()):
        stride = 1 << bit_pos
        moved = (
            shifted(tiles_a, "col", cols_axis - stride),
            shifted(for_sending(cols_a), "col", cols_axis - stride).astype(cols_a.dtype),
            shifted(for_sending(count_a), "col", cols_axis - stride).astype(count_a.dtype),
        )
        tiles_a, cols_a, count_a = select_if(
            row_group // stride % 2 == 1, moved, (tiles_a, cols_a, count_a)
        )
    for bit_pos in range((cols_axis - 1).bit_length()):
        stride = 1 << bit_pos
        nearby = stride % rows_axis
        if nearby:
            moved = (
                shifted(tiles_b, "row", rows_axis - nearby),
                shifted(for_sending(cols_b), "row", rows_axis - nearby).astype(cols_b.dtype),
                shifted(for_sending(count_b), "row", rows_axis - nearby).astype(count_b.dtype),
            )
        else:
            moved = (tiles_b, cols_b, count_b)
        moved = roll_slots(moved, (row_group + stride) // rows_axis)
        tiles_b, cols_b, count_b = select_if(
            col_group // stride % 2 == 1, moved, (tiles_b, cols_b, count_b)
        )
    tile_size = tiles_a.shape[2]
    running = jnp.zeros((tiles_a.shape[0], tile_size, BC * tile_size), jnp.float32)
    for turn_no in range(SHIFTS):
        current_tiles = tiles_b[0]
        current_cols = cols_b[0]
        current_count = count_b[0]
        rows_dense = dense_panel(current_tiles, current_cols, current_count, BC)
        running = running + panel_product(tiles_a, cols_a, count_a, rows_dense)
        if turn_no + 1 < SHIFTS:
            tiles_a, cols_a, count_a = (
                shifted(tiles_a, "col", cols_axis - 1),
                shifted(for_sending(cols_a), "col", cols_axis - 1).astype(cols_a.dtype),
                shifted(for_sending(count_a), "col", cols_axis - 1).astype(count_a.dtype),
            )
            moved = (
                shifted(tiles_b, "row", rows_axis - 1),
                shifted(for_sending(cols_b), "row", rows_axis - 1).astype(cols_b.dtype),
                shifted(for_sending(count_b), "row", rows_axis - 1).astype(count_b.dtype),
            )
            tiles_b, cols_b, count_b = roll_slots(moved, (row_group + 1) // rows_axis)
    flat_running = running.reshape(-1, running.shape[2])
    summed = lax.psum(flat_running, "depth")
    half_rows = flat_running.shape[0] // lax.axis_size("depth")
    own_rows = lax.dynamic_slice_in_dim(summed, lax.axis_index("depth") * half_rows, half_rows, 0)
    return own_rows.astype(jnp.bfloat16)


def solution(mesh):
    placed = (
        P("row", ("col", "depth"), None, None, None, None),
        P("row", ("col", "depth"), None, None),
        P("row", ("col", "depth"), None),
        P(None, "row", "depth", "col", None, None, None, None),
        P(None, "row", "depth", "col", None, None),
        P(None, "row", "depth", "col", None),
    )
    return jax.shard_map(
        local, mesh=mesh, in_specs=placed, out_specs=P(("row", "depth"), "col"), check_vma=False
    )
```

profile of v0, /device:TPU:0, one launch (start us, length us, event | category | flops | bytes accessed | tf_op | source)
XLA Modules:
  0.0 308.4 jit_solution(8262394096898452640)
XLA Ops:
  0.0 6.1 %collective-permute-start = (s32[8]{0:T(128)}, s32[8]{0:T(128)S(1)}, u32[]{:S(2)}, u32[]{:S(2)}) collective-permute-start(s32[8]{0:T(128)} %bitcast.190), channel_id=1, source_target_pairs={{0,14},{2,0},{4,2},{6,4},{8,6},{10,8},{12,10},{14,12},{1,15},{3,1}... | collective-permute-start | bytes 104 | tf_op jit(solution)/shard_map/ppermute | solution.py:18
  10.0 3.0 copy.31
  13.1 1.6 collective-permute-start.3
  15.4 6.1 %collective-permute-done.6 = s32[8]{0:T(128)S(1)} collective-permute-done((s32[8]{0:T(128)S(1)}, s32[8]{0:T(128)S(1)}, u32[]{:S(2)}, u32[]{:S(2)}) %collective-permute-start.6) | collective-permute-done | bytes 64 | tf_op jit(solution)/shard_map/ppermute | solution.py:18
  21.6 4.1 %collective-permute-start.12 = (s32[8]{0:T(128)S(1)}, s32[8]{0:T(128)S(1)}, u32[]{:S(2)}, u32[]{:S(2)}) collective-permute-start(s32[8]{0:T(128)S(1)} %collective-permute-done.6), channel_id=1, source_target_pairs={{0,14},{2,0},{4,2},{6,4},{8,6},{10,8},{12,10},{14,12},{1,15},{3,1}... | collective-permute-start | bytes 104 | tf_op jit(solution)/shard_map/ppermute | solution.py:18
  27.0 5.0 %collective-permute-start.18 = (s32[8]{0:T(128)S(1)}, s32[8]{0:T(128)S(1)}, u32[]{:S(2)}, u32[]{:S(2)}) collective-permute-start(s32[8]{0:T(128)S(1)} %collective-permute-done.12), channel_id=1, source_target_pairs={{0,14},{2,0},{4,2},{6,4},{8,6},{10,8},{12,10},{14,12},{1,15},{3,1}... | collective-permute-start | bytes 104 | tf_op jit(solution)/shard_map/ppermute | solution.py:18
  33.3 5.0 %collective-permute-start.8 = (s32[8,2]{0,1:T(2,128)S(1)}, s32[8,2]{0,1:T(2,128)S(1)}, u32[]{:S(2)}, u32[]{:S(2)}) collective-permute-start(s32[8,2]{0,1:T(2,128)S(1)} %broadcast_select_fusion.5), channel_id=1, source_target_pairs={{0,14},{2,0},{4,2},{6,4},{8,6},{10,8},{12,10},{14,12},{1,15},{3,1}... | collective-permute-start | bytes 200 | tf_op jit(solution)/shard_map/ppermute | solution.py:18
  39.6 5.0 %collective-permute-start.14 = (s32[8,2]{0,1:T(2,128)S(1)}, s32[8,2]{0,1:T(2,128)S(1)}, u32[]{:S(2)}, u32[]{:S(2)}) collective-permute-start(s32[8,2]{0,1:T(2,128)S(1)} %collective-permute-done.8), channel_id=1, source_target_pairs={{0,14},{2,0},{4,2},{6,4},{8,6},{10,8},{12,10},{14,12},{1,15},{3,1}... | collective-permute-start | bytes 200 | tf_op jit(solution)/shard_map/ppermute | solution.py:18
  45.9 5.0 %collective-permute-start.20 = (s32[8,2]{0,1:T(2,128)S(1)}, s32[8,2]{0,1:T(2,128)S(1)}, u32[]{:S(2)}, u32[]{:S(2)}) collective-permute-start(s32[8,2]{0,1:T(2,128)S(1)} %collective-permute-done.14), channel_id=1, source_target_pairs={{0,14},{2,0},{4,2},{6,4},{8,6},{10,8},{12,10},{14,12},{1,15},{3,1}... | collective-permute-start | bytes 200 | tf_op jit(solution)/shard_map/ppermute | solution.py:18
  51.0 1.6 collective-permute-start.10
  53.4 5.9 %collective-permute-done.10 = s32[4,16,1]{1,0,2:T(4,128)S(1)} collective-permute-done((s32[4,16,1]{1,0,2:T(4,128)S(1)}, s32[4,16,1]{1,0,2:T(4,128)S(1)}, u32[]{:S(2)}, u32[]{:S(2)}) %collective-permute-start.10) | collective-permute-done | bytes 288 | tf_op jit(solution)/shard_map/ppermute | solution.py:18
  68.3 11.7 %collective-permute-done.7 = bf16[8,2,128,128]{3,2,1,0:T(8,128)(2,1)S(1)} collective-permute-done((bf16[8,2,128,128]{3,2,1,0:T(8,128)(2,1)S(1)}, bf16[8,2,128,128]{3,2,1,0:T(8,128)(2,1)S(1)}, u32[]{:S(2)}, u32[]{:S(2)}) %collective-permute-start.7) | collective-permute-done | bytes 524320 | tf_op jit(solution)/shard_map/ppermute | solution.py:18
  81.6 12.1 %collective-permute-done.13 = bf16[8,2,128,128]{3,2,1,0:T(8,128)(2,1)S(1)} collective-permute-done((bf16[8,2,128,128]{3,2,1,0:T(8,128)(2,1)S(1)}, bf16[8,2,128,128]{3,2,1,0:T(8,128)(2,1)S(1)}, u32[]{:S(2)}, u32[]{:S(2)}) %collective-permute-start.13) | collective-permute-done | bytes 524320 | tf_op jit(solution)/shard_map/ppermute | solution.py:18
  95.1 2.4 fusion.47
  98.3 2.2 fusion.43
  102.0 2.2 fusion.51
  105.1 3.4 %broadcast.166.clone.2 = f32[2,4,128,1536]{3,2,1,0:T(8,128)} broadcast(f32[]{:T(128)} %constant.191.clone.1), dimensions={} | broadcast | bytes 6291460 | tf_op jit(solution)/shard_map/broadcast.11
  108.5 34.5 %while.44 = (s32[]{:T(128)}, f32[2,4,128,1536]{3,2,1,0:T(8,128)}, bf16[2,4,2,128,128]{4,3,2,1,0:T(8,128)(2,1)}, s32[2,4,2]{1,0,2:T(2,128)S(1)}, f32[16,12]{1,0:T(8,128)S(1)}, /*index=5*/f32[16,128,128]{1,2,0:T(8,128)}, s32[]{:T(128)}) while((s32[]{:T(128)}, f32[2,4,128,1536]{3,2,1,0:T(8,128)}, ...), condition=%wide.region_1.3_spmd.clone, body=%wide.region_0.2_spmd.clone.sunk | while | flops 410518592 | bytes 26482904 | solution.py:48
  108.8 5.0 %multiply_convert_fusion.8 = bf16[16,128,128,12]{1,2,3,0:T(8,128)(2,1)} fusion(f32[16,12]{1,0:T(8,128)S(1)} %get-tuple-element.488, f32[16,128,128]{1,2,0:T(8,128)} %get-tuple-element.489), kind=kLoop, calls=%fused_computation.8.clone.1 | loop fusion | flops 6291456 | bytes 7340800 | tf_op jit(solution)/shard_map/convert_element_type | solution.py:31
  113.8 5.4 %gather_fusion = bf16[8,128,1536]{1,2,0:T(8,128)(2,1)} fusion(bf16[16,128,1536]{1,2,0:T(8,128)(2,1)} %bitcast.162, s32[1024]{0:T(1024)S(1)} %pad_clamp_fusion.8), kind=kCustom, calls=%fused_computation.clone.clone.1 | custom fusion | bytes 6291488 | tf_op jit(solution)/shard_map/while/body/eval_jaxpr/jit(_take)/gather | solution.py:45
  119.2 3.2 %copy.57 = bf16[4,2,128,1536]{3,2,1,0:T(8,128)(2,1)S(1)} copy(bf16[4,2,128,1536]{2,3,1,0:T(8,128)(2,1)} %bitcast.166) | data formatting | bytes 6291456 | tf_op jit(solution)/shard_map/while/body/eval_jaxpr/jit(_take)/gather | solution.py:45
  122.4 3.4 %fusion.80 = f32[2,4,128,1536]{3,2,1,0:T(8,128)} fusion(f32[2,4,128,1536]{3,2,1,0:T(8,128)} %get-tuple-element.478, s32[]{:T(128)S(6)} %copy.86, bf16[4,2,128,1536]{3,2,1,0:T(8,128)(2,1)S(1)} %copy.57, pred[4,2]{1,0:T(4,128)(4,1)S(1)} %copy.58, bf16[2,4,2,128,128]{4,3,2,1,0:T(8,128)(2,1)} %get-tuple-element.486), kind=kOutput, calls=%fused_computation.10.clone.1 | convolution fusion | flops 404226048 | bytes 6554632 | tf_op jit(solution)/shard_map/while/body/eval_jaxpr/rtab,rtbn->ran/dot_general | solution.py:46
  126.1 5.0 %multiply_convert_fusion.8 = bf16[16,128,128,12]{1,2,3,0:T(8,128)(2,1)} fusion(f32[16,12]{1,0:T(8,128)S(1)} %get-tuple-element.488, f32[16,128,128]{1,2,0:T(8,128)} %get-tuple-element.489), kind=kLoop, calls=%fused_computation.8.clone.1 | loop fusion | flops 6291456 | bytes 7340800 | tf_op jit(solution)/shard_map/convert_element_type | solution.py:31
  131.0 5.4 %gather_fusion = bf16[8,128,1536]{1,2,0:T(8,128)(2,1)} fusion(bf16[16,128,1536]{1,2,0:T(8,128)(2,1)} %bitcast.162, s32[1024]{0:T(1024)S(1)} %pad_clamp_fusion.8), kind=kCustom, calls=%fused_computation.clone.clone.1 | custom fusion | bytes 6291488 | tf_op jit(solution)/shard_map/while/body/eval_jaxpr/jit(_take)/gather | solution.py:45
  136.5 3.2 %copy.57 = bf16[4,2,128,1536]{3,2,1,0:T(8,128)(2,1)S(1)} copy(bf16[4,2,128,1536]{2,3,1,0:T(8,128)(2,1)} %bitcast.166) | data formatting | bytes 6291456 | tf_op jit(solution)/shard_map/while/body/eval_jaxpr/jit(_take)/gather | solution.py:45
  139.7 3.4 %fusion.80 = f32[2,4,128,1536]{3,2,1,0:T(8,128)} fusion(f32[2,4,128,1536]{3,2,1,0:T(8,128)} %get-tuple-element.478, s32[]{:T(128)S(6)} %copy.86, bf16[4,2,128,1536]{3,2,1,0:T(8,128)(2,1)S(1)} %copy.57, pred[4,2]{1,0:T(4,128)(4,1)S(1)} %copy.58, bf16[2,4,2,128,128]{4,3,2,1,0:T(8,128)(2,1)} %get-tuple-element.486), kind=kOutput, calls=%fused_computation.10.clone.1 | convolution fusion | flops 404226048 | bytes 6554632 | tf_op jit(solution)/shard_map/while/body/eval_jaxpr/rtab,rtbn->ran/dot_general | solution.py:46
  143.0 3.7 %fusion.41 = bf16[4,16,1,128,128]{3,4,1,2,0:T(8,128)(2,1)} fusion(s32[]{:T(128)S(6)} %select_n.231, bf16[4,16,1,128,128]{3,4,1,2,0:T(8,128)(2,1)} %collective-permute-done.9), kind=kLoop, calls=%fused_computation.79 | loop fusion | flops 1048576 | bytes 4194308 | tf_op jit(solution)/shard_map/concatenate | solution.py:63
  146.8 2.1 fusion.50
  149.4 3.5 %broadcast.166.clone.3 = f32[2,4,128,1536]{3,2,1,0:T(8,128)} broadcast(f32[]{:T(128)} %constant.191.clone.1), dimensions={} | broadcast | bytes 6291460 | tf_op jit(solution)/shard_map/broadcast.11
  152.9 34.5 %while.45 = (s32[]{:T(128)}, f32[2,4,128,1536]{3,2,1,0:T(8,128)}, bf16[2,4,2,128,128]{4,3,2,1,0:T(8,128)(2,1)}, s32[2,4,2]{1,0,2:T(2,128)S(1)}, f32[16,12]{1,0:T(8,128)S(1)}, /*index=5*/f32[16,128,128]{1,2,0:T(8,128)}, s32[]{:T(128)}) while((s32[]{:T(128)}, f32[2,4,128,1536]{3,2,1,0:T(8,128)}, ...), condition=%wide.region_3.5_spmd.clone, body=%wide.region_2.4_spmd.clone.sunk | while | flops 410518592 | bytes 26482904 | solution.py:48
  153.2 4.9 %multiply_convert_fusion.9 = bf16[16,128,128,12]{1,2,3,0:T(8,128)(2,1)} fusion(f32[16,12]{1,0:T(8,128)S(1)} %get-tuple-element.509, f32[16,128,128]{1,2,0:T(8,128)} %get-tuple-element.510), kind=kLoop, calls=%fused_computation.22.clone.1 | loop fusion | flops 6291456 | bytes 7340800 | tf_op jit(solution)/shard_map/convert_element_type | solution.py:31
  158.1 5.4 %gather_fusion.1 = bf16[8,128,1536]{1,2,0:T(8,128)(2,1)} fusion(bf16[16,128,1536]{1,2,0:T(8,128)(2,1)} %bitcast.163, s32[1024]{0:T(1024)S(1)} %pad_clamp_fusion.9), kind=kCustom, calls=%fused_computation.1.clone.clone.1 | custom fusion | bytes 6291488 | tf_op jit(solution)/shard_map/while/body/eval_jaxpr/jit(_take)/gather | solution.py:45
  163.6 3.2 %copy.60 = bf16[4,2,128,1536]{3,2,1,0:T(8,128)(2,1)S(1)} copy(bf16[4,2,128,1536]{2,3,1,0:T(8,128)(2,1)} %bitcast.167) | data formatting | bytes 6291456 | tf_op jit(solution)/shard_map/while/body/eval_jaxpr/jit(_take)/gather | solution.py:45
  166.8 3.3 %fusion.83 = f32[2,4,128,1536]{3,2,1,0:T(8,128)} fusion(f32[2,4,128,1536]{3,2,1,0:T(8,128)} %get-tuple-element.499, s32[]{:T(128)S(6)} %copy.92, bf16[4,2,128,1536]{3,2,1,0:T(8,128)(2,1)S(1)} %copy.60, pred[4,2]{1,0:T(4,128)(4,1)S(1)} %copy.61, bf16[2,4,2,128,128]{4,3,2,1,0:T(8,128)(2,1)} %get-tuple-element.507), kind=kOutput, calls=%fused_computation.24.clone.1 | convolution fusion | flops 404226048 | bytes 6554632 | tf_op jit(solution)/shard_map/while/body/eval_jaxpr/rtab,rtbn->ran/dot_general | solution.py:46
  170.4 4.9 %multiply_convert_fusion.9 = bf16[16,128,128,12]{1,2,3,0:T(8,128)(2,1)} fusion(f32[16,12]{1,0:T(8,128)S(1)} %get-tuple-element.509, f32[16,128,128]{1,2,0:T(8,128)} %get-tuple-element.510), kind=kLoop, calls=%fused_computation.22.clone.1 | loop fusion | flops 6291456 | bytes 7340800 | tf_op jit(solution)/shard_map/convert_element_type | solution.py:31
  175.4 5.4 %gather_fusion.1 = bf16[8,128,1536]{1,2,0:T(8,128)(2,1)} fusion(bf16[16,128,1536]{1,2,0:T(8,128)(2,1)} %bitcast.163, s32[1024]{0:T(1024)S(1)} %pad_clamp_fusion.9), kind=kCustom, calls=%fused_computation.1.clone.clone.1 | custom fusion | bytes 6291488 | tf_op jit(solution)/shard_map/while/body/eval_jaxpr/jit(_take)/gather | solution.py:45
  180.8 3.2 %copy.60 = bf16[4,2,128,1536]{3,2,1,0:T(8,128)(2,1)S(1)} copy(bf16[4,2,128,1536]{2,3,1,0:T(8,128)(2,1)} %bitcast.167) | data formatting | bytes 6291456 | tf_op jit(solution)/shard_map/while/body/eval_jaxpr/jit(_take)/gather | solution.py:45
  184.0 3.4 %fusion.83 = f32[2,4,128,1536]{3,2,1,0:T(8,128)} fusion(f32[2,4,128,1536]{3,2,1,0:T(8,128)} %get-tuple-element.499, s32[]{:T(128)S(6)} %copy.92, bf16[4,2,128,1536]{3,2,1,0:T(8,128)(2,1)S(1)} %copy.60, pred[4,2]{1,0:T(4,128)(4,1)S(1)} %copy.61, bf16[2,4,2,128,128]{4,3,2,1,0:T(8,128)(2,1)} %get-tuple-element.507), kind=kOutput, calls=%fused_computation.24.clone.1 | convolution fusion | flops 404226048 | bytes 6554632 | tf_op jit(solution)/shard_map/while/body/eval_jaxpr/rtab,rtbn->ran/dot_general | solution.py:46
  187.7 3.7 %fusion.40 = bf16[4,16,1,128,128]{3,4,1,2,0:T(8,128)(2,1)} fusion(s32[]{:T(128)S(6)} %select_n.231, bf16[4,16,1,128,128]{3,4,1,2,0:T(8,128)(2,1)} %collective-permute-done.15), kind=kLoop, calls=%fused_computation.78 | loop fusion | flops 1048576 | bytes 4194308 | tf_op jit(solution)/shard_map/concatenate | solution.py:63
  191.4 2.1 fusion.49
  193.5 1.7 collective-permute-start.21
  195.2 3.4 %broadcast.166.clone.1 = f32[2,4,128,1536]{3,2,1,0:T(8,128)} broadcast(f32[]{:T(128)} %constant.191.clone.1), dimensions={} | broadcast | bytes 6291460 | tf_op jit(solution)/shard_map/broadcast.11
  198.6 34.5 %while.46 = (s32[]{:T(128)}, f32[2,4,128,1536]{3,2,1,0:T(8,128)}, bf16[2,4,2,128,128]{4,3,2,1,0:T(8,128)(2,1)}, s32[2,4,2]{1,0,2:T(2,128)S(1)}, f32[16,12]{1,0:T(8,128)S(1)}, /*index=5*/f32[16,128,128]{1,2,0:T(8,128)}, s32[]{:T(128)}) while((s32[]{:T(128)}, f32[2,4,128,1536]{3,2,1,0:T(8,128)}, ...), condition=%wide.region_5.7_spmd.clone, body=%wide.region_4.6_spmd.clone.sunk | while | flops 410518592 | bytes 26482904 | solution.py:48
  198.9 5.0 %multiply_convert_fusion.10 = bf16[16,128,128,12]{1,2,3,0:T(8,128)(2,1)} fusion(f32[16,12]{1,0:T(8,128)S(1)} %get-tuple-element.467, f32[16,128,128]{1,2,0:T(8,128)} %get-tuple-element.468), kind=kLoop, calls=%fused_computation.36.clone.1 | loop fusion | flops 6291456 | bytes 7340800 | tf_op jit(solution)/shard_map/convert_element_type | solution.py:31
  203.8 5.4 %gather_fusion.2 = bf16[8,128,1536]{1,2,0:T(8,128)(2,1)} fusion(bf16[16,128,1536]{1,2,0:T(8,128)(2,1)} %bitcast.164, s32[1024]{0:T(1024)S(1)} %pad_clamp_fusion.10), kind=kCustom, calls=%fused_computation.2.clone.clone.1 | custom fusion | bytes 6291488 | tf_op jit(solution)/shard_map/while/body/eval_jaxpr/jit(_take)/gather | solution.py:45
  209.3 3.2 %copy.63 = bf16[4,2,128,1536]{3,2,1,0:T(8,128)(2,1)S(1)} copy(bf16[4,2,128,1536]{2,3,1,0:T(8,128)(2,1)} %bitcast.168) | data formatting | bytes 6291456 | tf_op jit(solution)/shard_map/while/body/eval_jaxpr/jit(_take)/gather | solution.py:45
  212.5 3.3 %fusion.86 = f32[2,4,128,1536]{3,2,1,0:T(8,128)} fusion(f32[2,4,128,1536]{3,2,1,0:T(8,128)} %get-tuple-element.457, s32[]{:T(128)S(6)} %copy.80, bf16[4,2,128,1536]{3,2,1,0:T(8,128)(2,1)S(1)} %copy.63, pred[4,2]{1,0:T(4,128)(4,1)S(1)} %copy.64, bf16[2,4,2,128,128]{4,3,2,1,0:T(8,128)(2,1)} %get-tuple-element.465), kind=kOutput, calls=%fused_computation.38.clone.1 | convolution fusion | flops 404226048 | bytes 6554632 | tf_op jit(solution)/shard_map/while/body/eval_jaxpr/rtab,rtbn->ran/dot_general | solution.py:46
  216.1 5.0 %multiply_convert_fusion.10 = bf16[16,128,128,12]{1,2,3,0:T(8,128)(2,1)} fusion(f32[16,12]{1,0:T(8,128)S(1)} %get-tuple-element.467, f32[16,128,128]{1,2,0:T(8,128)} %get-tuple-element.468), kind=kLoop, calls=%fused_computation.36.clone.1 | loop fusion | flops 6291456 | bytes 7340800 | tf_op jit(solution)/shard_map/convert_element_type | solution.py:31
  221.1 5.4 %gather_fusion.2 = bf16[8,128,1536]{1,2,0:T(8,128)(2,1)} fusion(bf16[16,128,1536]{1,2,0:T(8,128)(2,1)} %bitcast.164, s32[1024]{0:T(1024)S(1)} %pad_clamp_fusion.10), kind=kCustom, calls=%fused_computation.2.clone.clone.1 | custom fusion | bytes 6291488 | tf_op jit(solution)/shard_map/while/body/eval_jaxpr/jit(_take)/gather | solution.py:45
  226.5 3.2 %copy.63 = bf16[4,2,128,1536]{3,2,1,0:T(8,128)(2,1)S(1)} copy(bf16[4,2,128,1536]{2,3,1,0:T(8,128)(2,1)} %bitcast.168) | data formatting | bytes 6291456 | tf_op jit(solution)/shard_map/while/body/eval_jaxpr/jit(_take)/gather | solution.py:45
  229.7 3.3 %fusion.86 = f32[2,4,128,1536]{3,2,1,0:T(8,128)} fusion(f32[2,4,128,1536]{3,2,1,0:T(8,128)} %get-tuple-element.457, s32[]{:T(128)S(6)} %copy.80, bf16[4,2,128,1536]{3,2,1,0:T(8,128)(2,1)S(1)} %copy.63, pred[4,2]{1,0:T(4,128)(4,1)S(1)} %copy.64, bf16[2,4,2,128,128]{4,3,2,1,0:T(8,128)(2,1)} %get-tuple-element.465), kind=kOutput, calls=%fused_computation.38.clone.1 | convolution fusion | flops 404226048 | bytes 6554632 | tf_op jit(solution)/shard_map/while/body/eval_jaxpr/rtab,rtbn->ran/dot_general | solution.py:46
  233.0 2.2 bitcast_convert_fusion
  235.3 3.4 %broadcast.166.clone = f32[2,4,128,1536]{3,2,1,0:T(8,128)} broadcast(f32[]{:T(128)} %constant.191.clone.1), dimensions={} | broadcast | bytes 6291460 | tf_op jit(solution)/shard_map/broadcast.11
  238.7 34.3 %while.47 = (s32[]{:T(128)}, f32[2,4,128,1536]{3,2,1,0:T(8,128)}, bf16[2,4,2,128,128]{4,3,2,1,0:T(8,128)(2,1)}, s32[2,4,2]{1,0,2:T(2,128)S(1)}, f32[16,12]{1,0:T(8,128)S(1)}, /*index=5*/f32[16,128,128]{1,2,0:T(8,128)}, s32[]{:T(128)}) while((s32[]{:T(128)}, f32[2,4,128,1536]{3,2,1,0:T(8,128)}, ...), condition=%wide.region_7.9_spmd.clone, body=%wide.region_6.8_spmd.clone.sunk | while | flops 410518592 | bytes 26482904 | solution.py:48
  239.0 4.9 %multiply_convert_fusion.11 = bf16[16,128,128,12]{1,2,3,0:T(8,128)(2,1)} fusion(f32[16,12]{1,0:T(8,128)S(1)} %get-tuple-element.446, f32[16,128,128]{1,2,0:T(8,128)} %get-tuple-element.447), kind=kLoop, calls=%fused_computation.50.clone.1 | loop fusion | flops 6291456 | bytes 7340800 | tf_op jit(solution)/shard_map/convert_element_type | solution.py:31
  243.9 5.4 %gather_fusion.3 = bf16[8,128,1536]{1,2,0:T(8,128)(2,1)} fusion(bf16[16,128,1536]{1,2,0:T(8,128)(2,1)} %bitcast.165, s32[1024]{0:T(1024)S(1)} %pad_clamp_fusion.11), kind=kCustom, calls=%fused_computation.3.clone.clone.1 | custom fusion | bytes 6291488 | tf_op jit(solution)/shard_map/while/body/eval_jaxpr/jit(_take)/gather | solution.py:45
  249.3 3.2 %copy.66 = bf16[4,2,128,1536]{3,2,1,0:T(8,128)(2,1)S(1)} copy(bf16[4,2,128,1536]{2,3,1,0:T(8,128)(2,1)} %bitcast.169) | data formatting | bytes 6291456 | tf_op jit(solution)/shard_map/while/body/eval_jaxpr/jit(_take)/gather | solution.py:45
  252.5 3.4 %fusion.89 = f32[2,4,128,1536]{3,2,1,0:T(8,128)} fusion(f32[2,4,128,1536]{3,2,1,0:T(8,128)} %get-tuple-element.436, s32[]{:T(128)S(6)} %copy.74, bf16[4,2,128,1536]{3,2,1,0:T(8,128)(2,1)S(1)} %copy.66, pred[4,2]{1,0:T(4,128)(4,1)S(1)} %copy.67, bf16[2,4,2,128,128]{4,3,2,1,0:T(8,128)(2,1)} %get-tuple-element.444), kind=kOutput, calls=%fused_computation.52.clone.1 | convolution fusion | flops 404226048 | bytes 6554632 | tf_op jit(solution)/shard_map/while/body/eval_jaxpr/rtab,rtbn->ran/dot_general | solution.py:46
  256.2 4.9 %multiply_convert_fusion.11 = bf16[16,128,128,12]{1,2,3,0:T(8,128)(2,1)} fusion(f32[16,12]{1,0:T(8,128)S(1)} %get-tuple-element.446, f32[16,128,128]{1,2,0:T(8,128)} %get-tuple-element.447), kind=kLoop, calls=%fused_computation.50.clone.1 | loop fusion | flops 6291456 | bytes 7340800 | tf_op jit(solution)/shard_map/convert_element_type | solution.py:31
  261.1 5.4 %gather_fusion.3 = bf16[8,128,1536]{1,2,0:T(8,128)(2,1)} fusion(bf16[16,128,1536]{1,2,0:T(8,128)(2,1)} %bitcast.165, s32[1024]{0:T(1024)S(1)} %pad_clamp_fusion.11), kind=kCustom, calls=%fused_computation.3.clone.clone.1 | custom fusion | bytes 6291488 | tf_op jit(solution)/shard_map/while/body/eval_jaxpr/jit(_take)/gather | solution.py:45
  266.5 3.2 %copy.66 = bf16[4,2,128,1536]{3,2,1,0:T(8,128)(2,1)S(1)} copy(bf16[4,2,128,1536]{2,3,1,0:T(8,128)(2,1)} %bitcast.169) | data formatting | bytes 6291456 | tf_op jit(solution)/shard_map/while/body/eval_jaxpr/jit(_take)/gather | solution.py:45
  269.6 3.4 %fusion.89 = f32[2,4,128,1536]{3,2,1,0:T(8,128)} fusion(f32[2,4,128,1536]{3,2,1,0:T(8,128)} %get-tuple-element.436, s32[]{:T(128)S(6)} %copy.74, bf16[4,2,128,1536]{3,2,1,0:T(8,128)(2,1)S(1)} %copy.66, pred[4,2]{1,0:T(4,128)(4,1)S(1)} %copy.67, bf16[2,4,2,128,128]{4,3,2,1,0:T(8,128)(2,1)} %get-tuple-element.444), kind=kOutput, calls=%fused_computation.52.clone.1 | convolution fusion | flops 404226048 | bytes 6554632 | tf_op jit(solution)/shard_map/while/body/eval_jaxpr/rtab,rtbn->ran/dot_general | solution.py:46
  273.0 13.8 %add_add_fusion = f32[2,4,128,1536]{3,2,1,0:T(8,128)} fusion(f32[2,4,128,1536]{3,2,1,0:T(8,128)} %get-tuple-element.117, f32[2,4,128,1536]{3,2,1,0:T(8,128)} %get-tuple-element.116, f32[2,4,128,1536]{3,2,1,0:T(8,128)} %get-tuple-element.114, f32[2,4,128,1536]{3,2,1,0:T(8,128)} %get-tuple-element.115), kind=kLoop, calls=%fused_computation.64 | loop fusion | flops 4718592 | bytes 31457280 | tf_op jit(solution)/shard_map/add | solution.py:117
  286.8 20.3 %all-reduce.1 = bf16[1024,1536]{1,0:T(8,128)(2,1)S(1)} all-reduce(f32[1024,1536]{1,0:T(8,128)} %bitcast.170), channel_id=1, replica_groups=mesh['row'=2,'col'=8,'depth'=2] {'depth'}, use_global_device_ids=true, to_apply=%region_8.10 | all-reduce | flops 1572864 | bytes 9437184 | tf_op jit(solution)/shard_map/psum | solution.py:131
  (153 shorter events, 30.7 us)
Async XLA Ops:
  0.0 14.7 %copy-start.4 = (s32[1,1,8]{2,1,0:T(1,128)S(1)}, s32[1,1,8]{2,1,0:T(1,128)}, u32[]{:S(2)}) copy-start(s32[1,1,8]{2,1,0:T(1,128)} %param.18) | copy-start | bytes 100
  0.0 15.3 %copy-start.3 = (s32[1,1,8,2]{2,3,1,0:T(2,128)S(1)}, s32[1,1,8,2]{2,3,1,0:T(2,128)}, u32[]{:S(2)}) copy-start(s32[1,1,8,2]{2,3,1,0:T(2,128)} %param.17) | copy-start | bytes 196
  0.0 50.9 %copy-start.1 = (s32[4,1,1,1,16,1]{4,5,3,2,1,0:T(1,128)S(1)}, s32[4,1,1,1,16,1]{4,5,3,2,1,0:T(1,128)}, u32[]{:S(2)}) copy-start(s32[4,1,1,1,16,1]{4,5,3,2,1,0:T(1,128)} %param.20) | copy-start | bytes 772
  0.0 52.6 %copy-start.2 = (s32[4,1,1,1,16]{4,3,2,1,0:T(1,128)S(1)}, s32[4,1,1,1,16]{4,3,2,1,0:T(1,128)}, u32[]{:S(2)}) copy-start(s32[4,1,1,1,16]{4,3,2,1,0:T(1,128)} %param.21) | copy-start | bytes 772
  0.0 66.7 %copy-start = (bf16[1,1,8,2,128,128]{5,4,3,2,1,0:T(8,128)(2,1)S(1)}, bf16[1,1,8,2,128,128]{5,4,3,2,1,0:T(8,128)(2,1)}, u32[]{:S(2)}) copy-start(bf16[1,1,8,2,128,128]{5,4,3,2,1,0:T(8,128)(2,1)} %param.16) | copy-start | bytes 1572868
  0.0 13.1 %collective-permute-start = (s32[8]{0:T(128)}, s32[8]{0:T(128)S(1)}, u32[]{:S(2)}, u32[]{:S(2)}) collective-permute-start(s32[8]{0:T(128)} %bitcast.190), channel_id=1, source_target_pairs={{0,14},{2,0},{4,2},{6,4},{8,6},{10,8},{12,10},{14,12},{1,15},{3,1}... | collective-permute-start | bytes 104 | tf_op jit(solution)/shard_map/ppermute | solution.py:18
  6.1 8.7 %collective-permute-start.2 = (s32[8,2]{0,1:T(2,128)}, s32[8,2]{0,1:T(2,128)S(1)}, u32[]{:S(2)}, u32[]{:S(2)}) collective-permute-start(s32[8,2]{0,1:T(2,128)} %bitcast.189), channel_id=1, source_target_pairs={{0,14},{2,0},{4,2},{6,4},{8,6},{10,8},{12,10},{14,12},{1,15},{3,1}... | collective-permute-start | bytes 200 | tf_op jit(solution)/shard_map/ppermute | solution.py:18
  6.6 44.3 %collective-permute-start.4 = (s32[4,16,1]{1,0,2:T(4,128)}, s32[4,16,1]{1,0,2:T(4,128)S(1)}, u32[]{:S(2)}, u32[]{:S(2)}) collective-permute-start(s32[4,16,1]{1,0,2:T(4,128)} %bitcast.185), channel_id=1, source_target_pairs={{0,16},{16,0},{1,17},{17,1},{2,18},{18,2},{3,19},{19,3},{4,20},{20... | collective-permute-start | bytes 776 | tf_op jit(solution)/shard_map/ppermute | solution.py:18
  8.1 44.4 %collective-permute-start.5 = (s32[4,16]{1,0:T(4,128)}, s32[4,16]{1,0:T(4,128)S(1)}, u32[]{:S(2)}, u32[]{:S(2)}) collective-permute-start(s32[4,16]{1,0:T(4,128)} %bitcast.187), channel_id=1, source_target_pairs={{0,16},{16,0},{1,17},{17,1},{2,18},{18,2},{3,19},{19,3},{4,20},{20... | collective-permute-start | bytes 776 | tf_op jit(solution)/shard_map/ppermute | solution.py:18
  8.6 58.0 %collective-permute-start.1 = (bf16[8,2,128,128]{3,2,1,0:T(8,128)(2,1)}, bf16[8,2,128,128]{3,2,1,0:T(8,128)(2,1)S(1)}, u32[]{:S(2)}, u32[]{:S(2)}) collective-permute-start(bf16[8,2,128,128]{3,2,1,0:T(8,128)(2,1)} %bitcast.176), channel_id=1, source_target_pairs={{0,14},{2,0},{4,2},{6,4},{8,6},{10,8},{12,10},{14,12},{1,15},{3,1}... | collective-permute-start | bytes 1572872 | tf_op jit(solution)/shard_map/ppermute | solution.py:18
  13.1 82.0 %collective-permute-start.3 = (bf16[4,16,1,128,128]{3,4,1,2,0:T(8,128)(2,1)S(1)}, bf16[4,16,1,128,128]{3,4,1,2,0:T(8,128)(2,1)}, u32[]{:S(2)}, u32[]{:S(2)}) collective-permute-start(bf16[4,16,1,128,128]{3,4,1,2,0:T(8,128)(2,1)S(1)} %bitcast.171), channel_id=1, source_target_pairs={{0,16},{16,0},{1,17},{17,1},{2,18},{18,2},{3,19},{19,3},{4,20},{20... | collective-permute-start | bytes 6291464 | tf_op jit(solution)/shard_map/ppermute | solution.py:18
  14.8 6.7 %collective-permute-start.6 = (s32[8]{0:T(128)S(1)}, s32[8]{0:T(128)S(1)}, u32[]{:S(2)}, u32[]{:S(2)}) collective-permute-start(s32[8]{0:T(128)S(1)} %broadcast_select_fusion.6), channel_id=1, source_target_pairs={{0,14},{2,0},{4,2},{6,4},{8,6},{10,8},{12,10},{14,12},{1,15},{3,1}... | collective-permute-start | bytes 104 | tf_op jit(solution)/shard_map/ppermute | solution.py:18
  21.6 5.4 %collective-permute-start.12 = (s32[8]{0:T(128)S(1)}, s32[8]{0:T(128)S(1)}, u32[]{:S(2)}, u32[]{:S(2)}) collective-permute-start(s32[8]{0:T(128)S(1)} %collective-permute-done.6), channel_id=1, source_target_pairs={{0,14},{2,0},{4,2},{6,4},{8,6},{10,8},{12,10},{14,12},{1,15},{3,1}... | collective-permute-start | bytes 104 | tf_op jit(solution)/shard_map/ppermute | solution.py:18
  27.0 6.3 %collective-permute-start.18 = (s32[8]{0:T(128)S(1)}, s32[8]{0:T(128)S(1)}, u32[]{:S(2)}, u32[]{:S(2)}) collective-permute-start(s32[8]{0:T(128)S(1)} %collective-permute-done.12), channel_id=1, source_target_pairs={{0,14},{2,0},{4,2},{6,4},{8,6},{10,8},{12,10},{14,12},{1,15},{3,1}... | collective-permute-start | bytes 104 | tf_op jit(solution)/shard_map/ppermute | solution.py:18
  33.3 6.3 %collective-permute-start.8 = (s32[8,2]{0,1:T(2,128)S(1)}, s32[8,2]{0,1:T(2,128)S(1)}, u32[]{:S(2)}, u32[]{:S(2)}) collective-permute-start(s32[8,2]{0,1:T(2,128)S(1)} %broadcast_select_fusion.5), channel_id=1, source_target_pairs={{0,14},{2,0},{4,2},{6,4},{8,6},{10,8},{12,10},{14,12},{1,15},{3,1}... | collective-permute-start | bytes 200 | tf_op jit(solution)/shard_map/ppermute | solution.py:18
  39.6 6.3 %collective-permute-start.14 = (s32[8,2]{0,1:T(2,128)S(1)}, s32[8,2]{0,1:T(2,128)S(1)}, u32[]{:S(2)}, u32[]{:S(2)}) collective-permute-start(s32[8,2]{0,1:T(2,128)S(1)} %collective-permute-done.8), channel_id=1, source_target_pairs={{0,14},{2,0},{4,2},{6,4},{8,6},{10,8},{12,10},{14,12},{1,15},{3,1}... | collective-permute-start | bytes 200 | tf_op jit(solution)/shard_map/ppermute | solution.py:18
  45.9 7.4 %collective-permute-start.20 = (s32[8,2]{0,1:T(2,128)S(1)}, s32[8,2]{0,1:T(2,128)S(1)}, u32[]{:S(2)}, u32[]{:S(2)}) collective-permute-start(s32[8,2]{0,1:T(2,128)S(1)} %collective-permute-done.14), channel_id=1, source_target_pairs={{0,14},{2,0},{4,2},{6,4},{8,6},{10,8},{12,10},{14,12},{1,15},{3,1}... | collective-permute-start | bytes 200 | tf_op jit(solution)/shard_map/ppermute | solution.py:18
  51.0 8.3 %collective-permute-start.10 = (s32[4,16,1]{1,0,2:T(4,128)S(1)}, s32[4,16,1]{1,0,2:T(4,128)S(1)}, u32[]{:S(2)}, u32[]{:S(2)}) collective-permute-start(s32[4,16,1]{1,0,2:T(4,128)S(1)} %fusion.62), channel_id=1, source_target_pairs={{0,16},{16,0},{1,17},{17,1},{2,18},{18,2},{3,19},{19,3},{4,20},{20... | collective-permute-start | bytes 776 | tf_op jit(solution)/shard_map/ppermute | solution.py:18
  52.7 8.2 %collective-permute-start.11 = (s32[4,16]{1,0:T(4,128)S(1)}, s32[4,16]{1,0:T(4,128)S(1)}, u32[]{:S(2)}, u32[]{:S(2)}) collective-permute-start(s32[4,16]{1,0:T(4,128)S(1)} %fusion.65), channel_id=1, source_target_pairs={{0,16},{16,0},{1,17},{17,1},{2,18},{18,2},{3,19},{19,3},{4,20},{20... | collective-permute-start | bytes 776 | tf_op jit(solution)/shard_map/ppermute | solution.py:18
  59.3 3.7 %collective-permute-start.16 = (s32[4,16,1]{1,0,2:T(4,128)S(1)}, s32[4,16,1]{1,0,2:T(4,128)S(1)}, u32[]{:S(2)}, u32[]{:S(2)}) collective-permute-start(s32[4,16,1]{1,0,2:T(4,128)S(1)} %constant_dynamic-slice_fusion.9), channel_id=1, source_target_pairs={{0,16},{16,0},{1,17},{17,1},{2,18},{18,2},{3,19},{19,3},{4,20},{20... | collective-permute-start | bytes 776 | tf_op jit(solution)/shard_map/ppermute | solution.py:18
  60.9 3.7 %collective-permute-start.17 = (s32[4,16]{1,0:T(4,128)S(1)}, s32[4,16]{1,0:T(4,128)S(1)}, u32[]{:S(2)}, u32[]{:S(2)}) collective-permute-start(s32[4,16]{1,0:T(4,128)S(1)} %constant_dynamic-slice_fusion.8), channel_id=1, source_target_pairs={{0,16},{16,0},{1,17},{17,1},{2,18},{18,2},{3,19},{19,3},{4,20},{20... | collective-permute-start | bytes 776 | tf_op jit(solution)/shard_map/ppermute | solution.py:18
  63.0 3.7 %collective-permute-start.22 = (s32[4,16,1]{1,0,2:T(4,128)S(1)}, s32[4,16,1]{1,0,2:T(4,128)S(1)}, u32[]{:S(2)}, u32[]{:S(2)}) collective-permute-start(s32[4,16,1]{1,0,2:T(4,128)S(1)} %constant_dynamic-slice_fusion.7), channel_id=1, source_target_pairs={{0,16},{16,0},{1,17},{17,1},{2,18},{18,2},{3,19},{19,3},{4,20},{20... | collective-permute-start | bytes 776 | tf_op jit(solution)/shard_map/ppermute | solution.py:18
  64.6 3.7 %collective-permute-start.23 = (s32[4,16]{1,0:T(4,128)S(1)}, s32[4,16]{1,0:T(4,128)S(1)}, u32[]{:S(2)}, u32[]{:S(2)}) collective-permute-start(s32[4,16]{1,0:T(4,128)S(1)} %constant_dynamic-slice_fusion.6), channel_id=1, source_target_pairs={{0,16},{16,0},{1,17},{17,1},{2,18},{18,2},{3,19},{19,3},{4,20},{20... | collective-permute-start | bytes 776 | tf_op jit(solution)/shard_map/ppermute | solution.py:18
  67.6 12.5 %collective-permute-start.7 = (bf16[8,2,128,128]{3,2,1,0:T(8,128)(2,1)S(1)}, bf16[8,2,128,128]{3,2,1,0:T(8,128)(2,1)S(1)}, u32[]{:S(2)}, u32[]{:S(2)}) collective-permute-start(bf16[8,2,128,128]{3,2,1,0:T(8,128)(2,1)S(1)} %get-tuple-element.279), channel_id=1, source_target_pairs={{0,14},{2,0},{4,2},{6,4},{8,6},{10,8},{12,10},{14,12},{1,15},{3,1}... | collective-permute-start | bytes 1572872 | tf_op jit(solution)/shard_map/ppermute | solution.py:18
  80.0 13.6 %collective-permute-start.13 = (bf16[8,2,128,128]{3,2,1,0:T(8,128)(2,1)S(1)}, bf16[8,2,128,128]{3,2,1,0:T(8,128)(2,1)S(1)}, u32[]{:S(2)}, u32[]{:S(2)}) collective-permute-start(bf16[8,2,128,128]{3,2,1,0:T(8,128)(2,1)S(1)} %collective-permute-done.7), channel_id=1, source_target_pairs={{0,14},{2,0},{4,2},{6,4},{8,6},{10,8},{12,10},{14,12},{1,15},{3,1}... | collective-permute-start | bytes 1572872 | tf_op jit(solution)/shard_map/ppermute | solution.py:18
  93.6 10.5 %collective-permute-start.19 = (bf16[8,2,128,128]{3,2,1,0:T(8,128)(2,1)S(1)}, bf16[8,2,128,128]{3,2,1,0:T(8,128)(2,1)S(1)}, u32[]{:S(2)}, u32[]{:S(2)}) collective-permute-start(bf16[8,2,128,128]{3,2,1,0:T(8,128)(2,1)S(1)} %collective-permute-done.13), channel_id=1, source_target_pairs={{0,14},{2,0},{4,2},{6,4},{8,6},{10,8},{12,10},{14,12},{1,15},{3,1}... | collective-permute-start | bytes 1572872 | tf_op jit(solution)/shard_map/ppermute | solution.py:18
  100.6 42.5 %collective-permute-start.9 = (bf16[4,16,1,128,128]{3,4,1,2,0:T(8,128)(2,1)}, bf16[4,16,1,128,128]{3,4,1,2,0:T(8,128)(2,1)}, u32[]{:S(2)}, u32[]{:S(2)}) collective-permute-start(bf16[4,16,1,128,128]{3,4,1,2,0:T(8,128)(2,1)} %fusion.43), channel_id=1, source_target_pairs={{0,16},{16,0},{1,17},{17,1},{2,18},{18,2},{3,19},{19,3},{4,20},{20... | collective-permute-start | bytes 6291464 | tf_op jit(solution)/shard_map/ppermute | solution.py:18
  148.9 38.8 %collective-permute-start.15 = (bf16[4,16,1,128,128]{3,4,1,2,0:T(8,128)(2,1)}, bf16[4,16,1,128,128]{3,4,1,2,0:T(8,128)(2,1)}, u32[]{:S(2)}, u32[]{:S(2)}) collective-permute-start(bf16[4,16,1,128,128]{3,4,1,2,0:T(8,128)(2,1)} %fusion.41), channel_id=1, source_target_pairs={{0,16},{16,0},{1,17},{17,1},{2,18},{18,2},{3,19},{19,3},{4,20},{20... | collective-permute-start | bytes 6291464 | tf_op jit(solution)/shard_map/ppermute | solution.py:18
  193.5 39.5 %collective-permute-start.21 = (bf16[4,16,1,128,128]{3,4,1,2,0:T(8,128)(2,1)}, bf16[4,16,1,128,128]{3,4,1,2,0:T(8,128)(2,1)}, u32[]{:S(2)}, u32[]{:S(2)}) collective-permute-start(bf16[4,16,1,128,128]{3,4,1,2,0:T(8,128)(2,1)} %fusion.40), channel_id=1, source_target_pairs={{0,16},{16,0},{1,17},{17,1},{2,18},{18,2},{3,19},{19,3},{4,20},{20... | collective-permute-start | bytes 6291464 | tf_op jit(solution)/shard_map/ppermute | solution.py:18
where the time goes:
time: 310 us; the launch traced here: 308 us
  local copies, waits for them, and re-layouts  89.5 us (29%)
  other arithmetic  79.5 us (26%)
  starting transfers between devices  47.8 us (15%)
  waiting for transfers between devices  44.1 us (14%)
  matrix products  26.8 us (9%)
  blocking collectives  20.3 us (7%)
    gather x16, local copies, waits for them, and re-layouts, one_group(): chosen = jnp.take(rows_dense, cols_part, axis=0)  68.8 us
    ppermute x24, starting transfers between devices, shifted(): return lax.ppermute(value, axis, pairs)  47.8 us
    ppermute x24, waiting for transfers between devices, shifted(): return lax.ppermute(value, axis, pairs)  44.1 us
    convert_element_type x8, other arithmetic, dense_panel(): spread.astype(jnp.bfloat16)  39.5 us
    dot_general x8, matrix products, one_group(): jnp.einsum('rtab,rtbn->ran', tiles_part, chosen, preferred_element_type=j...  26.8 us
    psum x1, blocking collectives, local(): summed = lax.psum(flat_running, 'depth')  20.3 us
    add x1, other arithmetic, local(): running = running + panel_product(tiles_a, cols_a, count_a, rows_dense)  13.8 us
    another operation x4, local copies, waits for them, and re-layouts  13.7 us
  transfers between devices with their start and end apart: 24, of which 12 were waited for; matrix products, arithmetic and copies ran while one was open for 42% of the time, Pallas kernels for 0%

commit v1 on v0

--- a/solution.py
+++ b/solution.py
@@ -128,7 +128,7 @@
             )
             tiles_b, cols_b, count_b = roll_slots(moved, (row_group + 1) // rows_axis)
     flat_running = running.reshape(-1, running.shape[2])
-    summed = lax.psum(flat_running, "depth")
+    summed = jnp.sum(lax.all_gather(flat_running, "depth"), axis=0)
     half_rows = flat_running.shape[0] // lax.axis_size("depth")
     own_rows = lax.dynamic_slice_in_dim(summed, lax.axis_index("depth") * half_rows, half_rows, 0)
     return own_rows.astype(jnp.bfloat16)

time: 310 us -> 346 us (1.12)
  blocking collectives: 20.3 us -> 0 us
  starting transfers between devices: 47.8 us -> 66.1 us
  waiting for transfers between devices: 44.1 us -> 62.1 us
  between operations: 0.27 us -> 13.6 us
  other arithmetic: 79.5 us -> 85.9 us
    all_gather x0 -> x1, waiting for transfers between devices: none -> 23.5 us  [local(): summed = jnp.sum(lax.all_gather(flat_running, 'depth'), axis=0)]
    psum x1 -> x0, blocking collectives: 20.3 us -> none  [local(): summed = lax.psum(flat_running, 'depth')]
    ppermute x24, starting transfers between devices: 47.8 us -> 66 us  [shifted(): return lax.ppermute(value, axis, pairs)]
    reduce_sum x0 -> x1, other arithmetic: none -> 6.57 us  [local(): summed = jnp.sum(lax.all_gather(flat_running, 'depth'), axis=0)]
    ppermute x24, waiting for transfers between devices: 44.1 us -> 38.7 us  [shifted(): return lax.ppermute(value, axis, pairs)]
  transfers between devices with their start and end apart: 24 -> 25, of which waited for: 12 -> 15; matrix products, arithmetic and copies ran while one was open for 42% -> 37% of each run, Pallas kernels for 0% -> 0%
where the time goes in v1:
time: 346 us; the launch traced here: 344 us
  local copies, waits for them, and re-layouts  89.6 us (26%)
  other arithmetic  85.9 us (25%)
  starting transfers between devices  66.1 us (19%)
  waiting for transfers between devices  62.1 us (18%)
  matrix products  26.8 us (8%)
  between operations  13.6 us (4%)
    gather x16, local copies, waits for them, and re-layouts, one_group(): chosen = jnp.take(rows_dense, cols_part, axis=0)  68.7 us
    ppermute x24, starting transfers between devices, shifted(): return lax.ppermute(value, axis, pairs)  66 us
    convert_element_type x8, other arithmetic, dense_panel(): spread.astype(jnp.bfloat16)  39.5 us
    ppermute x24, waiting for transfers between devices, shifted(): return lax.ppermute(value, axis, pairs)  38.7 us
    dot_general x8, matrix products, one_group(): jnp.einsum('rtab,rtbn->ran', tiles_part, chosen, preferred_element_type=j...  26.8 us
    all_gather x1, waiting for transfers between devices, local(): summed = jnp.sum(lax.all_gather(flat_running, 'depth'), axis=0)  23.5 us
    add x1, other arithmetic, local(): running = running + panel_product(tiles_a, cols_a, count_a, rows_dense)  13.8 us
    another operation x4, local copies, waits for them, and re-layouts  13.7 us
  transfers between devices with their start and end apart: 25, of which 15 were waited for; matrix products, arithmetic and copies ran while one was open for 37% of the time, Pallas kernels for 0%

profile of v1, /device:TPU:0, one launch (start us, length us, event | category | flops | bytes accessed | tf_op | source)
XLA Modules:
  0.0 344.3 jit_solution(11527402594995335450)
XLA Ops:
  6.6 3.1 copy.48
  9.7 3.1 collective-permute-start.3
  14.8 4.5 %collective-permute-start = (s32[8]{0:T(128)S(1)}, s32[8]{0:T(128)S(1)}, u32[]{:S(2)}, u32[]{:S(2)}) collective-permute-start(s32[8]{0:T(128)S(1)} %bitcast.190), channel_id=1, source_target_pairs={{0,14},{2,0},{4,2},{6,4},{8,6},{10,8},{12,10},{14,12},{1,15},{3,1}... | collective-permute-start | bytes 104 | tf_op jit(solution)/shard_map/ppermute | solution.py:18
  20.7 5.0 %collective-permute-start.2 = (s32[8,2]{0,1:T(2,128)S(1)}, s32[8,2]{0,1:T(2,128)S(1)}, u32[]{:S(2)}, u32[]{:S(2)}) collective-permute-start(s32[8,2]{0,1:T(2,128)S(1)} %bitcast.189), channel_id=1, source_target_pairs={{0,14},{2,0},{4,2},{6,4},{8,6},{10,8},{12,10},{14,12},{1,15},{3,1}... | collective-permute-start | bytes 200 | tf_op jit(solution)/shard_map/ppermute | solution.py:18
  25.7 6.3 %collective-permute-done.2 = s32[8,2]{0,1:T(2,128)S(1)} collective-permute-done((s32[8,2]{0,1:T(2,128)S(1)}, s32[8,2]{0,1:T(2,128)S(1)}, u32[]{:S(2)}, u32[]{:S(2)}) %collective-permute-start.2) | collective-permute-done | bytes 96 | tf_op jit(solution)/shard_map/ppermute | solution.py:18
  32.0 3.2 collective-permute-start.6
  36.6 5.0 %collective-permute-start.12 = (s32[8]{0:T(128)S(1)}, s32[8]{0:T(128)S(1)}, u32[]{:S(2)}, u32[]{:S(2)}) collective-permute-start(s32[8]{0:T(128)S(1)} %collective-permute-done.6), channel_id=1, source_target_pairs={{0,14},{2,0},{4,2},{6,4},{8,6},{10,8},{12,10},{14,12},{1,15},{3,1}... | collective-permute-start | bytes 104 | tf_op jit(solution)/shard_map/ppermute | solution.py:18
  42.8 5.0 %collective-permute-start.8 = (s32[8,2]{0,1:T(2,128)S(1)}, s32[8,2]{0,1:T(2,128)S(1)}, u32[]{:S(2)}, u32[]{:S(2)}) collective-permute-start(s32[8,2]{0,1:T(2,128)S(1)} %broadcast_select_fusion.5), channel_id=1, source_target_pairs={{0,14},{2,0},{4,2},{6,4},{8,6},{10,8},{12,10},{14,12},{1,15},{3,1}... | collective-permute-start | bytes 200 | tf_op jit(solution)/shard_map/ppermute | solution.py:18
  49.1 5.0 %collective-permute-start.18 = (s32[8]{0:T(128)S(1)}, s32[8]{0:T(128)S(1)}, u32[]{:S(2)}, u32[]{:S(2)}) collective-permute-start(s32[8]{0:T(128)S(1)} %collective-permute-done.12), channel_id=1, source_target_pairs={{0,14},{2,0},{4,2},{6,4},{8,6},{10,8},{12,10},{14,12},{1,15},{3,1}... | collective-permute-start | bytes 104 | tf_op jit(solution)/shard_map/ppermute | solution.py:18
  55.4 5.0 %collective-permute-start.14 = (s32[8,2]{0,1:T(2,128)S(1)}, s32[8,2]{0,1:T(2,128)S(1)}, u32[]{:S(2)}, u32[]{:S(2)}) collective-permute-start(s32[8,2]{0,1:T(2,128)S(1)} %collective-permute-done.8), channel_id=1, source_target_pairs={{0,14},{2,0},{4,2},{6,4},{8,6},{10,8},{12,10},{14,12},{1,15},{3,1}... | collective-permute-start | bytes 200 | tf_op jit(solution)/shard_map/ppermute | solution.py:18
  61.7 5.0 %collective-permute-start.20 = (s32[8,2]{0,1:T(2,128)S(1)}, s32[8,2]{0,1:T(2,128)S(1)}, u32[]{:S(2)}, u32[]{:S(2)}) collective-permute-start(s32[8,2]{0,1:T(2,128)S(1)} %collective-permute-done.14), channel_id=1, source_target_pairs={{0,14},{2,0},{4,2},{6,4},{8,6},{10,8},{12,10},{14,12},{1,15},{3,1}... | collective-permute-start | bytes 200 | tf_op jit(solution)/shard_map/ppermute | solution.py:18
  78.7 2.6 collective-permute-start.7
  81.4 11.6 %collective-permute-done.7 = bf16[8,2,128,128]{3,2,1,0:T(8,128)(2,1)S(1)} collective-permute-done((bf16[8,2,128,128]{3,2,1,0:T(8,128)(2,1)S(1)}, bf16[8,2,128,128]{3,2,1,0:T(8,128)(2,1)S(1)}, u32[]{:S(2)}, u32[]{:S(2)}) %collective-permute-start.7) | collective-permute-done | bytes 524320 | tf_op jit(solution)/shard_map/ppermute | solution.py:18
  93.0 5.2 %collective-permute-start.13 = (bf16[8,2,128,128]{3,2,1,0:T(8,128)(2,1)S(1)}, bf16[8,2,128,128]{3,2,1,0:T(8,128)(2,1)S(1)}, u32[]{:S(2)}, u32[]{:S(2)}) collective-permute-start(bf16[8,2,128,128]{3,2,1,0:T(8,128)(2,1)S(1)} %collective-permute-done.7), channel_id=1, source_target_pairs={{0,14},{2,0},{4,2},{6,4},{8,6},{10,8},{12,10},{14,12},{1,15},{3,1}... | collective-permute-start | bytes 1572872 | tf_op jit(solution)/shard_map/ppermute | solution.py:18
  99.2 9.8 %collective-permute-done.13 = bf16[8,2,128,128]{3,2,1,0:T(8,128)(2,1)S(1)} collective-permute-done((bf16[8,2,128,128]{3,2,1,0:T(8,128)(2,1)S(1)}, bf16[8,2,128,128]{3,2,1,0:T(8,128)(2,1)S(1)}, u32[]{:S(2)}, u32[]{:S(2)}) %collective-permute-start.13) | collective-permute-done | bytes 524320 | tf_op jit(solution)/shard_map/ppermute | solution.py:18
  109.0 5.2 %collective-permute-start.19 = (bf16[8,2,128,128]{3,2,1,0:T(8,128)(2,1)S(1)}, bf16[8,2,128,128]{3,2,1,0:T(8,128)(2,1)S(1)}, u32[]{:S(2)}, u32[]{:S(2)}) collective-permute-start(bf16[8,2,128,128]{3,2,1,0:T(8,128)(2,1)S(1)} %collective-permute-done.13), channel_id=1, source_target_pairs={{0,14},{2,0},{4,2},{6,4},{8,6},{10,8},{12,10},{14,12},{1,15},{3,1}... | collective-permute-start | bytes 1572872 | tf_op jit(solution)/shard_map/ppermute | solution.py:18
  115.1 2.4 fusion.47
  118.4 2.2 fusion.43
  125.1 3.4 broadcast.166.clone.2
  128.5 34.6 %while.44 = (s32[]{:T(128)}, f32[2,4,128,1536]{3,2,1,0:T(8,128)}, bf16[2,4,2,128,128]{4,3,2,1,0:T(8,128)(2,1)}, s32[2,4,2]{1,0,2:T(2,128)S(1)}, f32[16,12]{1,0:T(8,128)S(1)}, /*index=5*/f32[16,128,128]{1,2,0:T(8,128)}, s32[]{:T(128)}) while((s32[]{:T(128)}, f32[2,4,128,1536]{3,2,1,0:T(8,128)}, ...), condition=%wide.region_1.3_spmd.clone, body=%wide.region_0.2_spmd.clone.sunk | while | flops 410518592 | bytes 26482896 | solution.py:48
  128.7 4.9 %multiply_convert_fusion.8 = bf16[16,128,128,12]{1,2,3,0:T(8,128)(2,1)} fusion(f32[16,12]{1,0:T(8,128)S(1)} %get-tuple-element.512, f32[16,128,128]{1,2,0:T(8,128)} %get-tuple-element.513), kind=kLoop, calls=%fused_computation.8.clone.1 | loop fusion | flops 6291456 | bytes 7340800 | tf_op jit(solution)/shard_map/convert_element_type | solution.py:31
  133.7 5.5 %gather_fusion = bf16[8,128,1536]{1,2,0:T(8,128)(2,1)} fusion(bf16[16,128,1536]{1,2,0:T(8,128)(2,1)} %bitcast.162, s32[1024]{0:T(1024)S(1)} %pad_clamp_fusion.8), kind=kCustom, calls=%fused_computation.clone.clone.1 | custom fusion | bytes 6291488 | tf_op jit(solution)/shard_map/while/body/eval_jaxpr/jit(_take)/gather | solution.py:45
  139.1 3.2 copy.74
  142.4 3.4 fusion.80
  146.0 4.9 %multiply_convert_fusion.8 = bf16[16,128,128,12]{1,2,3,0:T(8,128)(2,1)} fusion(f32[16,12]{1,0:T(8,128)S(1)} %get-tuple-element.512, f32[16,128,128]{1,2,0:T(8,128)} %get-tuple-element.513), kind=kLoop, calls=%fused_computation.8.clone.1 | loop fusion | flops 6291456 | bytes 7340800 | tf_op jit(solution)/shard_map/convert_element_type | solution.py:31
  151.0 5.5 %gather_fusion = bf16[8,128,1536]{1,2,0:T(8,128)(2,1)} fusion(bf16[16,128,1536]{1,2,0:T(8,128)(2,1)} %bitcast.162, s32[1024]{0:T(1024)S(1)} %pad_clamp_fusion.8), kind=kCustom, calls=%fused_computation.clone.clone.1 | custom fusion | bytes 6291488 | tf_op jit(solution)/shard_map/while/body/eval_jaxpr/jit(_take)/gather | solution.py:45
  156.4 3.2 copy.74
  159.7 3.4 fusion.80
  163.1 3.7 %fusion.41 = bf16[4,16,1,128,128]{3,4,1,2,0:T(8,128)(2,1)} fusion(s32[]{:T(128)S(6)} %select_n.231, bf16[4,16,1,128,128]{3,4,1,2,0:T(8,128)(2,1)} %collective-permute-done.9), kind=kLoop, calls=%fused_computation.79 | loop fusion | flops 1048576 | bytes 4194308 | tf_op jit(solution)/shard_map/concatenate | solution.py:63
  169.5 3.5 %broadcast.166.clone.3 = f32[2,4,128,1536]{3,2,1,0:T(8,128)} broadcast(f32[]{:T(128)} %constant.192.clone.1), dimensions={} | broadcast | bytes 6291460 | tf_op jit(solution)/shard_map/broadcast.11
  173.0 34.5 %while.45 = (s32[]{:T(128)}, f32[2,4,128,1536]{3,2,1,0:T(8,128)}, bf16[2,4,2,128,128]{4,3,2,1,0:T(8,128)(2,1)}, s32[2,4,2]{1,0,2:T(2,128)S(1)}, f32[16,12]{1,0:T(8,128)S(1)}, /*index=5*/f32[16,128,128]{1,2,0:T(8,128)}, s32[]{:T(128)}) while((s32[]{:T(128)}, f32[2,4,128,1536]{3,2,1,0:T(8,128)}, ...), condition=%wide.region_3.5_spmd.clone, body=%wide.region_2.4_spmd.clone.sunk | while | flops 410518592 | bytes 26482896 | solution.py:48
  173.2 4.9 %multiply_convert_fusion.9 = bf16[16,128,128,12]{1,2,3,0:T(8,128)(2,1)} fusion(f32[16,12]{1,0:T(8,128)S(1)} %get-tuple-element.533, f32[16,128,128]{1,2,0:T(8,128)} %get-tuple-element.534), kind=kLoop, calls=%fused_computation.22.clone.1 | loop fusion | flops 6291456 | bytes 7340800 | tf_op jit(solution)/shard_map/convert_element_type | solution.py:31
  178.1 5.5 %gather_fusion.1 = bf16[8,128,1536]{1,2,0:T(8,128)(2,1)} fusion(bf16[16,128,1536]{1,2,0:T(8,128)(2,1)} %bitcast.163, s32[1024]{0:T(1024)S(1)} %pad_clamp_fusion.9), kind=kCustom, calls=%fused_computation.1.clone.clone.1 | custom fusion | bytes 6291488 | tf_op jit(solution)/shard_map/while/body/eval_jaxpr/jit(_take)/gather | solution.py:45
  183.6 3.2 copy.77
  186.9 3.3 fusion.83
  190.4 4.9 %multiply_convert_fusion.9 = bf16[16,128,128,12]{1,2,3,0:T(8,128)(2,1)} fusion(f32[16,12]{1,0:T(8,128)S(1)} %get-tuple-element.533, f32[16,128,128]{1,2,0:T(8,128)} %get-tuple-element.534), kind=kLoop, calls=%fused_computation.22.clone.1 | loop fusion | flops 6291456 | bytes 7340800 | tf_op jit(solution)/shard_map/convert_element_type | solution.py:31
  195.3 5.5 %gather_fusion.1 = bf16[8,128,1536]{1,2,0:T(8,128)(2,1)} fusion(bf16[16,128,1536]{1,2,0:T(8,128)(2,1)} %bitcast.163, s32[1024]{0:T(1024)S(1)} %pad_clamp_fusion.9), kind=kCustom, calls=%fused_computation.1.clone.clone.1 | custom fusion | bytes 6291488 | tf_op jit(solution)/shard_map/while/body/eval_jaxpr/jit(_take)/gather | solution.py:45
  200.8 3.2 copy.77
  204.1 3.3 fusion.83
  207.4 3.7 %fusion.40 = bf16[4,16,1,128,128]{3,4,1,2,0:T(8,128)(2,1)} fusion(s32[]{:T(128)S(6)} %select_n.231, bf16[4,16,1,128,128]{3,4,1,2,0:T(8,128)(2,1)} %collective-permute-done.15), kind=kLoop, calls=%fused_computation.78 | loop fusion | flops 1048576 | bytes 4194308 | tf_op jit(solution)/shard_map/concatenate | solution.py:63
  214.7 3.4 broadcast.166.clone.1
  218.1 34.4 %while.46 = (s32[]{:T(128)}, f32[2,4,128,1536]{3,2,1,0:T(8,128)}, bf16[2,4,2,128,128]{4,3,2,1,0:T(8,128)(2,1)}, s32[2,4,2]{1,0,2:T(2,128)S(1)}, f32[16,12]{1,0:T(8,128)S(1)}, /*index=5*/f32[16,128,128]{1,2,0:T(8,128)}, s32[]{:T(128)}) while((s32[]{:T(128)}, f32[2,4,128,1536]{3,2,1,0:T(8,128)}, ...), condition=%wide.region_5.7_spmd.clone, body=%wide.region_4.6_spmd.clone.sunk | while | flops 410518592 | bytes 26482896 | solution.py:48
  218.3 4.9 %multiply_convert_fusion.10 = bf16[16,128,128,12]{1,2,3,0:T(8,128)(2,1)} fusion(f32[16,12]{1,0:T(8,128)S(1)} %get-tuple-element.491, f32[16,128,128]{1,2,0:T(8,128)} %get-tuple-element.492), kind=kLoop, calls=%fused_computation.36.clone.1 | loop fusion | flops 6291456 | bytes 7340800 | tf_op jit(solution)/shard_map/convert_element_type | solution.py:31
  223.2 5.4 %gather_fusion.2 = bf16[8,128,1536]{1,2,0:T(8,128)(2,1)} fusion(bf16[16,128,1536]{1,2,0:T(8,128)(2,1)} %bitcast.164, s32[1024]{0:T(1024)S(1)} %pad_clamp_fusion.10), kind=kCustom, calls=%fused_computation.2.clone.clone.1 | custom fusion | bytes 6291488 | tf_op jit(solution)/shard_map/while/body/eval_jaxpr/jit(_take)/gather | solution.py:45
  228.6 3.2 copy.80
  231.9 3.4 fusion.86
  235.5 4.9 %multiply_convert_fusion.10 = bf16[16,128,128,12]{1,2,3,0:T(8,128)(2,1)} fusion(f32[16,12]{1,0:T(8,128)S(1)} %get-tuple-element.491, f32[16,128,128]{1,2,0:T(8,128)} %get-tuple-element.492), kind=kLoop, calls=%fused_computation.36.clone.1 | loop fusion | flops 6291456 | bytes 7340800 | tf_op jit(solution)/shard_map/convert_element_type | solution.py:31
  240.4 5.4 %gather_fusion.2 = bf16[8,128,1536]{1,2,0:T(8,128)(2,1)} fusion(bf16[16,128,1536]{1,2,0:T(8,128)(2,1)} %bitcast.164, s32[1024]{0:T(1024)S(1)} %pad_clamp_fusion.10), kind=kCustom, calls=%fused_computation.2.clone.clone.1 | custom fusion | bytes 6291488 | tf_op jit(solution)/shard_map/while/body/eval_jaxpr/jit(_take)/gather | solution.py:45
  245.8 3.2 copy.80
  249.1 3.4 fusion.86
  252.5 2.2 bitcast_convert_fusion
  254.7 3.4 broadcast.166.clone
  258.1 34.2 %while.47 = (s32[]{:T(128)}, f32[2,4,128,1536]{3,2,1,0:T(8,128)}, bf16[2,4,2,128,128]{4,3,2,1,0:T(8,128)(2,1)}, s32[2,4,2]{1,0,2:T(2,128)S(1)}, f32[16,12]{1,0:T(8,128)S(1)}, /*index=5*/f32[16,128,128]{1,2,0:T(8,128)}, s32[]{:T(128)}) while((s32[]{:T(128)}, f32[2,4,128,1536]{3,2,1,0:T(8,128)}, ...), condition=%wide.region_7.9_spmd.clone, body=%wide.region_6.8_spmd.clone.sunk | while | flops 410518592 | bytes 26482896 | solution.py:48
  258.3 4.9 %multiply_convert_fusion.11 = bf16[16,128,128,12]{1,2,3,0:T(8,128)(2,1)} fusion(f32[16,12]{1,0:T(8,128)S(1)} %get-tuple-element.470, f32[16,128,128]{1,2,0:T(8,128)} %get-tuple-element.471), kind=kLoop, calls=%fused_computation.50.clone.1 | loop fusion | flops 6291456 | bytes 7340800 | tf_op jit(solution)/shard_map/convert_element_type | solution.py:31
  263.2 5.4 %gather_fusion.3 = bf16[8,128,1536]{1,2,0:T(8,128)(2,1)} fusion(bf16[16,128,1536]{1,2,0:T(8,128)(2,1)} %bitcast.165, s32[1024]{0:T(1024)S(1)} %pad_clamp_fusion.11), kind=kCustom, calls=%fused_computation.3.clone.clone.1 | custom fusion | bytes 6291488 | tf_op jit(solution)/shard_map/while/body/eval_jaxpr/jit(_take)/gather | solution.py:45
  268.6 3.2 copy.83
  271.9 3.3 fusion.89
  275.4 4.9 %multiply_convert_fusion.11 = bf16[16,128,128,12]{1,2,3,0:T(8,128)(2,1)} fusion(f32[16,12]{1,0:T(8,128)S(1)} %get-tuple-element.470, f32[16,128,128]{1,2,0:T(8,128)} %get-tuple-element.471), kind=kLoop, calls=%fused_computation.50.clone.1 | loop fusion | flops 6291456 | bytes 7340800 | tf_op jit(solution)/shard_map/convert_element_type | solution.py:31
  280.3 5.4 %gather_fusion.3 = bf16[8,128,1536]{1,2,0:T(8,128)(2,1)} fusion(bf16[16,128,1536]{1,2,0:T(8,128)(2,1)} %bitcast.165, s32[1024]{0:T(1024)S(1)} %pad_clamp_fusion.11), kind=kCustom, calls=%fused_computation.3.clone.clone.1 | custom fusion | bytes 6291488 | tf_op jit(solution)/shard_map/while/body/eval_jaxpr/jit(_take)/gather | solution.py:45
  285.7 3.2 copy.83
  289.0 3.4 fusion.89
  292.3 13.8 %add_add_fusion = f32[2,4,128,1536]{3,2,1,0:T(8,128)} fusion(f32[2,4,128,1536]{3,2,1,0:T(8,128)} %get-tuple-element.117, f32[2,4,128,1536]{3,2,1,0:T(8,128)} %get-tuple-element.116, f32[2,4,128,1536]{3,2,1,0:T(8,128)} %get-tuple-element.114, f32[2,4,128,1536]{3,2,1,0:T(8,128)} %get-tuple-element.115), kind=kLoop, calls=%fused_computation.64 | loop fusion | flops 4718592 | bytes 31457280 | tf_op jit(solution)/shard_map/add | solution.py:117
  306.2 23.5 %all-gather.2.cloned.1.call-done = f32[2,1024,1536]{2,1,0:T(8,128)} async-done(((f32[1,1024,1536]{2,1,0:T(8,128)}), f32[2,1024,1536]{2,1,0:T(8,128)}) %all-gather.2.cloned.1.call-update) | async-done | bytes 12582928 | tf_op jit(solution)/shard_map/all_gather | solution.py:131
  329.6 6.6 %reduce_sum.9 = bf16[1024,1536]{1,0:T(8,128)(2,1)S(1)} reduce(f32[2,1024,1536]{2,1,0:T(8,128)} %all-gather.2.cloned.1.call-done, f32[]{:T(128)} %constant.192.clone.1), dimensions={0}, to_apply=%region_8.10 | reduce | flops 1572864 | bytes 15728644 | tf_op jit(solution)/shard_map/reduce_sum | solution.py:131
  (156 shorter events, 39.2 us)
Async XLA Ops:
  6.5 6.3 %copy-start.1 = (s32[4,1,1,1,16]{4,3,2,1,0:T(1,128)S(1)}, s32[4,1,1,1,16]{4,3,2,1,0:T(1,128)}, u32[]{:S(2)}) copy-start(s32[4,1,1,1,16]{4,3,2,1,0:T(1,128)} %param.21) | copy-start | bytes 772
  6.5 6.3 %copy-start.2 = (s32[4,1,1,1,16,1]{4,5,3,2,1,0:T(1,128)S(1)}, s32[4,1,1,1,16,1]{4,5,3,2,1,0:T(1,128)}, u32[]{:S(2)}) copy-start(s32[4,1,1,1,16,1]{4,5,3,2,1,0:T(1,128)} %param.20) | copy-start | bytes 772
  6.5 8.3 %copy-start.4 = (s32[1,1,8]{2,1,0:T(1,128)S(1)}, s32[1,1,8]{2,1,0:T(1,128)}, u32[]{:S(2)}) copy-start(s32[1,1,8]{2,1,0:T(1,128)} %param.18) | copy-start | bytes 100
  6.5 12.8 %copy-start = (bf16[1,1,8,2,128,128]{5,4,3,2,1,0:T(8,128)(2,1)S(1)}, bf16[1,1,8,2,128,128]{5,4,3,2,1,0:T(8,128)(2,1)}, u32[]{:S(2)}) copy-start(bf16[1,1,8,2,128,128]{5,4,3,2,1,0:T(8,128)(2,1)} %param.16) | copy-start | bytes 1572868
  6.5 14.1 %copy-start.3 = (s32[1,1,8,2]{2,3,1,0:T(2,128)S(1)}, s32[1,1,8,2]{2,3,1,0:T(2,128)}, u32[]{:S(2)}) copy-start(s32[1,1,8,2]{2,3,1,0:T(2,128)} %param.17) | copy-start | bytes 196
  6.5 323.1 %all-gather.2.cloned.1.call-start = ((), (), s32[]{:S(2)}) async-start(), calls=%async_computation | async-start | bytes 18874368 | tf_op jit(solution)/shard_map/all_gather | solution.py:131
  9.7 105.4 %collective-permute-start.3 = (bf16[4,16,1,128,128]{3,4,1,2,0:T(8,128)(2,1)S(1)}, bf16[4,16,1,128,128]{3,4,1,2,0:T(8,128)(2,1)}, u32[]{:S(2)}, u32[]{:S(2)}) collective-permute-start(bf16[4,16,1,128,128]{3,4,1,2,0:T(8,128)(2,1)S(1)} %bitcast.171), channel_id=1, source_target_pairs={{0,16},{16,0},{1,17},{17,1},{2,18},{18,2},{3,19},{19,3},{4,20},{20... | collective-permute-start | bytes 6291464 | tf_op jit(solution)/shard_map/ppermute | solution.py:18
  12.8 53.9 %collective-permute-start.5 = (s32[4,16]{1,0:T(4,128)S(1)}, s32[4,16]{1,0:T(4,128)S(1)}, u32[]{:S(2)}, u32[]{:S(2)}) collective-permute-start(s32[4,16]{1,0:T(4,128)S(1)} %bitcast.185), channel_id=1, source_target_pairs={{0,16},{16,0},{1,17},{17,1},{2,18},{18,2},{3,19},{19,3},{4,20},{20... | collective-permute-start | bytes 776 | tf_op jit(solution)/shard_map/ppermute | solution.py:18
  12.9 54.5 %collective-permute-start.4 = (s32[4,16,1]{1,0,2:T(4,128)S(1)}, s32[4,16,1]{1,0,2:T(4,128)S(1)}, u32[]{:S(2)}, u32[]{:S(2)}) collective-permute-start(s32[4,16,1]{1,0,2:T(4,128)S(1)} %bitcast.187), channel_id=1, source_target_pairs={{0,16},{16,0},{1,17},{17,1},{2,18},{18,2},{3,19},{19,3},{4,20},{20... | collective-permute-start | bytes 776 | tf_op jit(solution)/shard_map/ppermute | solution.py:18
  14.8 5.8 %collective-permute-start = (s32[8]{0:T(128)S(1)}, s32[8]{0:T(128)S(1)}, u32[]{:S(2)}, u32[]{:S(2)}) collective-permute-start(s32[8]{0:T(128)S(1)} %bitcast.190), channel_id=1, source_target_pairs={{0,14},{2,0},{4,2},{6,4},{8,6},{10,8},{12,10},{14,12},{1,15},{3,1}... | collective-permute-start | bytes 104 | tf_op jit(solution)/shard_map/ppermute | solution.py:18
  19.4 58.5 %collective-permute-start.1 = (bf16[8,2,128,128]{3,2,1,0:T(8,128)(2,1)S(1)}, bf16[8,2,128,128]{3,2,1,0:T(8,128)(2,1)S(1)}, u32[]{:S(2)}, u32[]{:S(2)}) collective-permute-start(bf16[8,2,128,128]{3,2,1,0:T(8,128)(2,1)S(1)} %bitcast.176), channel_id=1, source_target_pairs={{0,14},{2,0},{4,2},{6,4},{8,6},{10,8},{12,10},{14,12},{1,15},{3,1}... | collective-permute-start | bytes 1572872 | tf_op jit(solution)/shard_map/ppermute | solution.py:18
  20.7 11.3 %collective-permute-start.2 = (s32[8,2]{0,1:T(2,128)S(1)}, s32[8,2]{0,1:T(2,128)S(1)}, u32[]{:S(2)}, u32[]{:S(2)}) collective-permute-start(s32[8,2]{0,1:T(2,128)S(1)} %bitcast.189), channel_id=1, source_target_pairs={{0,14},{2,0},{4,2},{6,4},{8,6},{10,8},{12,10},{14,12},{1,15},{3,1}... | collective-permute-start | bytes 200 | tf_op jit(solution)/shard_map/ppermute | solution.py:18
  32.0 4.5 %collective-permute-start.6 = (s32[8]{0:T(128)S(1)}, s32[8]{0:T(128)S(1)}, u32[]{:S(2)}, u32[]{:S(2)}) collective-permute-start(s32[8]{0:T(128)S(1)} %broadcast_select_fusion.6), channel_id=1, source_target_pairs={{0,14},{2,0},{4,2},{6,4},{8,6},{10,8},{12,10},{14,12},{1,15},{3,1}... | collective-permute-start | bytes 104 | tf_op jit(solution)/shard_map/ppermute | solution.py:18
  36.6 6.3 %collective-permute-start.12 = (s32[8]{0:T(128)S(1)}, s32[8]{0:T(128)S(1)}, u32[]{:S(2)}, u32[]{:S(2)}) collective-permute-start(s32[8]{0:T(128)S(1)} %collective-permute-done.6), channel_id=1, source_target_pairs={{0,14},{2,0},{4,2},{6,4},{8,6},{10,8},{12,10},{14,12},{1,15},{3,1}... | collective-permute-start | bytes 104 | tf_op jit(solution)/shard_map/ppermute | solution.py:18
  42.8 6.3 %collective-permute-start.8 = (s32[8,2]{0,1:T(2,128)S(1)}, s32[8,2]{0,1:T(2,128)S(1)}, u32[]{:S(2)}, u32[]{:S(2)}) collective-permute-start(s32[8,2]{0,1:T(2,128)S(1)} %broadcast_select_fusion.5), channel_id=1, source_target_pairs={{0,14},{2,0},{4,2},{6,4},{8,6},{10,8},{12,10},{14,12},{1,15},{3,1}... | collective-permute-start | bytes 200 | tf_op jit(solution)/shard_map/ppermute | solution.py:18
  49.1 6.3 %collective-permute-start.18 = (s32[8]{0:T(128)S(1)}, s32[8]{0:T(128)S(1)}, u32[]{:S(2)}, u32[]{:S(2)}) collective-permute-start(s32[8]{0:T(128)S(1)} %collective-permute-done.12), channel_id=1, source_target_pairs={{0,14},{2,0},{4,2},{6,4},{8,6},{10,8},{12,10},{14,12},{1,15},{3,1}... | collective-permute-start | bytes 104 | tf_op jit(solution)/shard_map/ppermute | solution.py:18
  55.4 6.3 %collective-permute-start.14 = (s32[8,2]{0,1:T(2,128)S(1)}, s32[8,2]{0,1:T(2,128)S(1)}, u32[]{:S(2)}, u32[]{:S(2)}) collective-permute-start(s32[8,2]{0,1:T(2,128)S(1)} %collective-permute-done.8), channel_id=1, source_target_pairs={{0,14},{2,0},{4,2},{6,4},{8,6},{10,8},{12,10},{14,12},{1,15},{3,1}... | collective-permute-start | bytes 200 | tf_op jit(solution)/shard_map/ppermute | solution.py:18
  61.7 7.4 %collective-permute-start.20 = (s32[8,2]{0,1:T(2,128)S(1)}, s32[8,2]{0,1:T(2,128)S(1)}, u32[]{:S(2)}, u32[]{:S(2)}) collective-permute-start(s32[8,2]{0,1:T(2,128)S(1)} %collective-permute-done.14), channel_id=1, source_target_pairs={{0,14},{2,0},{4,2},{6,4},{8,6},{10,8},{12,10},{14,12},{1,15},{3,1}... | collective-permute-start | bytes 200 | tf_op jit(solution)/shard_map/ppermute | solution.py:18
  66.8 3.7 %collective-permute-start.11 = (s32[4,16]{1,0:T(4,128)S(1)}, s32[4,16]{1,0:T(4,128)S(1)}, u32[]{:S(2)}, u32[]{:S(2)}) collective-permute-start(s32[4,16]{1,0:T(4,128)S(1)} %fusion.65), channel_id=1, source_target_pairs={{0,16},{16,0},{1,17},{17,1},{2,18},{18,2},{3,19},{19,3},{4,20},{20... | collective-permute-start | bytes 776 | tf_op jit(solution)/shard_map/ppermute | solution.py:18
  67.5 3.7 %collective-permute-start.10 = (s32[4,16,1]{1,0,2:T(4,128)S(1)}, s32[4,16,1]{1,0,2:T(4,128)S(1)}, u32[]{:S(2)}, u32[]{:S(2)}) collective-permute-start(s32[4,16,1]{1,0,2:T(4,128)S(1)} %fusion.62), channel_id=1, source_target_pairs={{0,16},{16,0},{1,17},{17,1},{2,18},{18,2},{3,19},{19,3},{4,20},{20... | collective-permute-start | bytes 776 | tf_op jit(solution)/shard_map/ppermute | solution.py:18
  70.5 3.7 %collective-permute-start.17 = (s32[4,16]{1,0:T(4,128)S(1)}, s32[4,16]{1,0:T(4,128)S(1)}, u32[]{:S(2)}, u32[]{:S(2)}) collective-permute-start(s32[4,16]{1,0:T(4,128)S(1)} %constant_dynamic-slice_fusion.8), channel_id=1, source_target_pairs={{0,16},{16,0},{1,17},{17,1},{2,18},{18,2},{3,19},{19,3},{4,20},{20... | collective-permute-start | bytes 776 | tf_op jit(solution)/shard_map/ppermute | solution.py:18
  71.2 3.7 %collective-permute-start.16 = (s32[4,16,1]{1,0,2:T(4,128)S(1)}, s32[4,16,1]{1,0,2:T(4,128)S(1)}, u32[]{:S(2)}, u32[]{:S(2)}) collective-permute-start(s32[4,16,1]{1,0,2:T(4,128)S(1)} %constant_dynamic-slice_fusion.9), channel_id=1, source_target_pairs={{0,16},{16,0},{1,17},{17,1},{2,18},{18,2},{3,19},{19,3},{4,20},{20... | collective-permute-start | bytes 776 | tf_op jit(solution)/shard_map/ppermute | solution.py:18
  74.2 3.7 %collective-permute-start.23 = (s32[4,16]{1,0:T(4,128)S(1)}, s32[4,16]{1,0:T(4,128)S(1)}, u32[]{:S(2)}, u32[]{:S(2)}) collective-permute-start(s32[4,16]{1,0:T(4,128)S(1)} %constant_dynamic-slice_fusion.6), channel_id=1, source_target_pairs={{0,16},{16,0},{1,17},{17,1},{2,18},{18,2},{3,19},{19,3},{4,20},{20... | collective-permute-start | bytes 776 | tf_op jit(solution)/shard_map/ppermute | solution.py:18
  74.8 6.5 %collective-permute-start.22 = (s32[4,16,1]{1,0,2:T(4,128)S(1)}, s32[4,16,1]{1,0,2:T(4,128)S(1)}, u32[]{:S(2)}, u32[]{:S(2)}) collective-permute-start(s32[4,16,1]{1,0,2:T(4,128)S(1)} %constant_dynamic-slice_fusion.7), channel_id=1, source_target_pairs={{0,16},{16,0},{1,17},{17,1},{2,18},{18,2},{3,19},{19,3},{4,20},{20... | collective-permute-start | bytes 776 | tf_op jit(solution)/shard_map/ppermute | solution.py:18
  78.7 14.3 %collective-permute-start.7 = (bf16[8,2,128,128]{3,2,1,0:T(8,128)(2,1)S(1)}, bf16[8,2,128,128]{3,2,1,0:T(8,128)(2,1)S(1)}, u32[]{:S(2)}, u32[]{:S(2)}) collective-permute-start(bf16[8,2,128,128]{3,2,1,0:T(8,128)(2,1)S(1)} %get-tuple-element.303), channel_id=1, source_target_pairs={{0,14},{2,0},{4,2},{6,4},{8,6},{10,8},{12,10},{14,12},{1,15},{3,1}... | collective-permute-start | bytes 1572872 | tf_op jit(solution)/shard_map/ppermute | solution.py:18
  93.0 16.0 %collective-permute-start.13 = (bf16[8,2,128,128]{3,2,1,0:T(8,128)(2,1)S(1)}, bf16[8,2,128,128]{3,2,1,0:T(8,128)(2,1)S(1)}, u32[]{:S(2)}, u32[]{:S(2)}) collective-permute-start(bf16[8,2,128,128]{3,2,1,0:T(8,128)(2,1)S(1)} %collective-permute-done.7), channel_id=1, source_target_pairs={{0,14},{2,0},{4,2},{6,4},{8,6},{10,8},{12,10},{14,12},{1,15},{3,1}... | collective-permute-start | bytes 1572872 | tf_op jit(solution)/shard_map/ppermute | solution.py:18
  109.0 15.1 %collective-permute-start.19 = (bf16[8,2,128,128]{3,2,1,0:T(8,128)(2,1)S(1)}, bf16[8,2,128,128]{3,2,1,0:T(8,128)(2,1)S(1)}, u32[]{:S(2)}, u32[]{:S(2)}) collective-permute-start(bf16[8,2,128,128]{3,2,1,0:T(8,128)(2,1)S(1)} %collective-permute-done.13), channel_id=1, source_target_pairs={{0,14},{2,0},{4,2},{6,4},{8,6},{10,8},{12,10},{14,12},{1,15},{3,1}... | collective-permute-start | bytes 1572872 | tf_op jit(solution)/shard_map/ppermute | solution.py:18
  120.6 42.5 %collective-permute-start.9 = (bf16[4,16,1,128,128]{3,4,1,2,0:T(8,128)(2,1)}, bf16[4,16,1,128,128]{3,4,1,2,0:T(8,128)(2,1)}, u32[]{:S(2)}, u32[]{:S(2)}) collective-permute-start(bf16[4,16,1,128,128]{3,4,1,2,0:T(8,128)(2,1)} %fusion.43), channel_id=1, source_target_pairs={{0,16},{16,0},{1,17},{17,1},{2,18},{18,2},{3,19},{19,3},{4,20},{20... | collective-permute-start | bytes 6291464 | tf_op jit(solution)/shard_map/ppermute | solution.py:18
  169.0 38.5 %collective-permute-start.15 = (bf16[4,16,1,128,128]{3,4,1,2,0:T(8,128)(2,1)}, bf16[4,16,1,128,128]{3,4,1,2,0:T(8,128)(2,1)}, u32[]{:S(2)}, u32[]{:S(2)}) collective-permute-start(bf16[4,16,1,128,128]{3,4,1,2,0:T(8,128)(2,1)} %fusion.41), channel_id=1, source_target_pairs={{0,16},{16,0},{1,17},{17,1},{2,18},{18,2},{3,19},{19,3},{4,20},{20... | collective-permute-start | bytes 6291464 | tf_op jit(solution)/shard_map/ppermute | solution.py:18
  213.2 39.2 %collective-permute-start.21 = (bf16[4,16,1,128,128]{3,4,1,2,0:T(8,128)(2,1)}, bf16[4,16,1,128,128]{3,4,1,2,0:T(8,128)(2,1)}, u32[]{:S(2)}, u32[]{:S(2)}) collective-permute-start(bf16[4,16,1,128,128]{3,4,1,2,0:T(8,128)(2,1)} %fusion.40), channel_id=1, source_target_pairs={{0,16},{16,0},{1,17},{17,1},{2,18},{18,2},{3,19},{19,3},{4,20},{20... | collective-permute-start | bytes 6291464 | tf_op jit(solution)/shard_map/ppermute | solution.py:18
Sparse Core Ops, SparseCore 0:
  306.3 23.2 all-gather.1
